TPU v7x, 32 devices: a whole 2x2x4 slice. The times are simulated.
32 devices in a mesh: seq: 4 (over x, core), fsdp: 8 (over z, y).
Axes of the slice: x: 2, y: 2, z: 4, core: 2. Of those that a mesh axis runs over, the one named last changes fastest.
Arguments:
- hidden_in: bfloat16 [8, 512, 1024], P('fsdp', 'seq'), may hold values from -6 to 6
- grad_out: bfloat16 [8, 512, 1024], P('fsdp', 'seq'), may hold values from -6 to 6
- segments: int32 [8, 512], P('fsdp'), may hold values from 0 to 1, as said below
- norm_gain: bfloat16 [1024], P('fsdp'), may hold values from 0.5 to 1.5
- mamba_in: bfloat16 [1024, 3328], P('fsdp'), may hold values from -0.1875 to 0.1875
- step_in: bfloat16 [1024, 24], P('fsdp'), may hold values from -0.1875 to 0.1875
- attn_in: bfloat16 [1024, 768], P('fsdp'), may hold values from -0.1875 to 0.1875
- conv_taps: float32 [4, 1792], replicated, may hold values from -3 to 3
- conv_bias: float32 [1792], replicated, may hold values from -1.75 to 1.75
- step_bias: float32 [24], replicated, may hold values from -2 to 0.5
- log_decay: float32 [24], replicated, may hold values from -7 to -2.5
- skip_gain: float32 [24], replicated, may hold values from 0.5 to 1.5
- gated_gain: bfloat16 [1536], P('fsdp'), may hold values from 0.5 to 1.5
- mamba_out: bfloat16 [1536, 1024], P('fsdp'), may hold values from -0.15625 to 0.15625
- attn_out: bfloat16 [512, 1024], P('fsdp'), may hold values from -0.75 to 0.75
- ffn_gain: bfloat16 [1024], P('fsdp'), may hold values from 0.5 to 1.5
- gate_up: bfloat16 [1024, 4096], P('fsdp'), may hold values from -0.1875 to 0.1875
- down_proj: bfloat16 [2048, 1024], P('fsdp'), may hold values from -0.125 to 0.125
Outputs:
- hidden_out: bfloat16 [8, 512, 1024], P('fsdp', 'seq')
- grad_in: float32 [8, 512, 1024], P('fsdp', 'seq')
- grad_norm_gain: float32 [1024], P('fsdp')
- grad_mamba_in: float32 [1024, 3328], P('fsdp')
- grad_step_in: float32 [1024, 24], P('fsdp')
- grad_attn_in: float32 [1024, 768], P('fsdp')
- grad_conv_taps: float32 [4, 1792], replicated
- grad_conv_bias: float32 [1792], replicated
- grad_step_bias: float32 [24], replicated
- grad_log_decay: float32 [24], replicated
- grad_skip_gain: float32 [24], replicated
- grad_gated_gain: float32 [1536], P('fsdp')
- grad_mamba_out: float32 [1536, 1024], P('fsdp')
- grad_attn_out: float32 [512, 1024], P('fsdp')
- grad_ffn_gain: float32 [1024], P('fsdp')
- grad_gate_up: float32 [1024, 4096], P('fsdp')
- grad_down_proj: float32 [2048, 1024], P('fsdp')
Inputs may be any that keep to these rules, and one draw needn't show every extreme that they name: `segments`: in each pack the ids are 0 up to some position and 1 from there on: a pack holds one sequence or two, the first at least 128 tokens long.
All inputs are finite; a program needn't handle non-finite values.
Results may differ from a plain program's by a relative error of at most 0.015.
Values may be sent and summed in bfloat16 or wider, within the bound.
A program may use at most 192 MiB of HBM per device.

v0:
```python
from functools import partial
import math

import jax
import jax.numpy as jnp
from jax import lax
from jax.sharding import PartitionSpec as P

MH = 24
HD = 64
NST = 128
KC = 4
QH = 8
KVH = 2
FF = 2048
SPAN = 128
DI = 1536


EPS = 1e-05
ROPE_THETA = 10000.0


def rms_scale(values):
    return lax.rsqrt(jnp.mean(values * values, axis=-1, keepdims=True) + EPS)


def swish_slope(values):
    sigma = jax.nn.sigmoid(values)
    return sigma * (1.0 + values * (1.0 - sigma))


def scan_blocks(x_heads, b_mat, c_mat, step, log_step, seg_ids):
    row_count, head_count, width = x_heads.shape
    state = b_mat.shape[1]
    block_count = row_count // SPAN
    highest = lax.Precision.HIGHEST
    spots = jnp.arange(SPAN, dtype=jnp.int32)
    causal = spots[:, None] >= spots[None, :]

    def one_block(carry, items):
        state_in, prev_seg = carry
        x_blk, b_blk, c_blk, step_blk, log_blk, seg_blk = items
        local = jnp.cumsum(log_blk, axis=0)
        inside = causal & (seg_blk[:, None] == seg_blk[None, :])
        inner = jnp.dot(c_blk, b_blk.T, precision=highest)
        local_t = local.T
        expo = jnp.where(inside[None], local_t[:, :, None] - local_t[:, None, :], -1e30)
        mixing = inner[None] * jnp.exp(expo) * step_blk.T[:, None, :]
        intra = jnp.einsum("htp,phd->thd", mixing, x_blk, precision=highest)
        carried = jnp.einsum("tn,hnd->thd", c_blk, state_in, precision=highest)
        lead = jnp.where((seg_blk == prev_seg)[:, None], jnp.exp(local), 0.0)
        out_blk = intra + lead[:, :, None] * carried
        last_seg = seg_blk[SPAN - 1]
        tail = jnp.where(
            (seg_blk == last_seg)[:, None],
            jnp.exp(local[SPAN - 1][None, :] - local) * step_blk,
            0.0,
        )
        fresh = jnp.einsum("ph,pn,phd->hnd", tail, b_blk, x_blk, precision=highest)
        keep = jnp.where(prev_seg == last_seg, jnp.exp(local[SPAN - 1]), 0.0)
        state_out = keep[:, None, None] * state_in + fresh
        return ((state_out, last_seg), out_blk)

    start = (jnp.zeros((head_count, state, width), x_heads.dtype), jnp.int32(-1))
    items = (
        x_heads.reshape(block_count, SPAN, head_count, width),
        b_mat.reshape(block_count, SPAN, state),
        c_mat.reshape(block_count, SPAN, state),
        step.reshape(block_count, SPAN, head_count),
        log_step.reshape(block_count, SPAN, head_count),
        seg_ids.reshape(block_count, SPAN),
    )
    final, outputs = lax.scan(one_block, start, items)
    return outputs.reshape(row_count, head_count, width)


def mixer_core(
    xs_in,
    bc_in,
    step_raw,
    query_in,
    kv_in,
    seg_ids,
    taps,
    tap_bias,
    step_bias,
    log_decay,
    skip_gain,
):
    row_count = xs_in.shape[0]
    head_count = step_raw.shape[1]
    width = xs_in.shape[1] // head_count
    state = bc_in.shape[1] // 2
    highest = lax.Precision.HIGHEST
    pre_conv = jnp.concatenate([xs_in, bc_in], axis=1)
    tap_count = taps.shape[0]
    accum = tap_bias[None, :] + taps[tap_count - 1][None, :] * pre_conv
    for lag_step in range(1, tap_count):
        moved = jnp.concatenate(
            [
                jnp.zeros((lag_step, pre_conv.shape[1]), pre_conv.dtype),
                pre_conv[: row_count - lag_step],
            ],
            axis=0,
        )
        prior = jnp.concatenate(
            [jnp.full((lag_step,), -1, jnp.int32), seg_ids[: row_count - lag_step]]
        )
        same_seq = (prior == seg_ids)[:, None]
        accum = accum + taps[tap_count - 1 - lag_step][None, :] * jnp.where(same_seq, moved, 0.0)
    activated = jax.nn.silu(accum)
    x_heads = activated[:, : head_count * width].reshape(row_count, head_count, width)
    b_mat = activated[:, head_count * width : head_count * width + state]
    c_mat = activated[:, head_count * width + state :]
    step = jax.nn.softplus(step_raw + step_bias[None, :])
    log_step = -jnp.exp(log_decay)[None, :] * step
    ssm_out = (
        scan_blocks(x_heads, b_mat, c_mat, step, log_step, seg_ids)
        + skip_gain[None, :, None] * x_heads
    )
    positions = jnp.arange(row_count, dtype=jnp.int32)
    mask = (positions[:, None] >= positions[None, :]) & (seg_ids[:, None] == seg_ids[None, :])
    query_count = query_in.shape[1] // width
    kv_count = kv_in.shape[1] // (2 * width)
    group_size = query_count // kv_count
    place = (jnp.sum(mask.astype(jnp.int32), axis=1) - 1).astype(xs_in.dtype)
    half = width // 2
    freqs = jnp.exp(-math.log(ROPE_THETA) * 2.0 * jnp.arange(half, dtype=xs_in.dtype) / width)
    angles = place[:, None] * freqs[None, :]
    cosine = jnp.cos(angles)[:, None, :]
    sine = jnp.sin(angles)[:, None, :]

    def rotate(tensor):
        first_half = tensor[..., :half]
        second_half = tensor[..., half:]
        return jnp.concatenate(
            [first_half * cosine - second_half * sine, second_half * cosine + first_half * sine],
            axis=-1,
        )

    queries = rotate(query_in.reshape(row_count, query_count, width)).reshape(
        row_count, kv_count, group_size, width
    )
    kv_pair = kv_in.reshape(row_count, kv_count, 2, width)
    keys = rotate(kv_pair[:, :, 0])
    values = kv_pair[:, :, 1]
    scores = jnp.einsum("ikgp,jkp->kgij", queries, keys, precision=highest) * (
        1.0 / math.sqrt(width)
    )
    scores = jnp.where(mask[None, None], scores, -1e30)
    weights = jnp.exp(scores)
    weights = weights / jnp.sum(weights, axis=-1, keepdims=True)
    attended = jnp.einsum("kgij,jkp->ikgp", weights, values, precision=highest)
    return (
        ssm_out.reshape(row_count, head_count * width),
        attended.reshape(row_count, query_count * width),
    )


def core_apply(seg_ids, inputs, params):
    return mixer_core(*inputs, seg_ids, *params)


def shards(
    hidden_in,
    grad_out,
    segments,
    norm_gain,
    mamba_in,
    step_in,
    attn_in,
    conv_taps,
    conv_bias,
    step_bias,
    log_decay,
    skip_gain,
    gated_gain,
    mamba_out,
    attn_out,
    ffn_gain,
    gate_up,
    down_proj,
):
    bf_type = jnp.bfloat16
    fl_type = jnp.float32
    seq_count = lax.axis_size("seq")
    seq_index = lax.axis_index("seq")
    block_rows = hidden_in.shape[1]
    x_width = DI // seq_count
    head_share = MH // seq_count
    owners = [group * KVH // seq_count for group in range(seq_count)]
    gathered = (
        lax.all_gather(norm_gain, "fsdp", axis=0, tiled=True),
        lax.all_gather(gated_gain, "fsdp", axis=0, tiled=True),
        lax.all_gather(ffn_gain, "fsdp", axis=0, tiled=True),
        lax.all_gather(mamba_in, "fsdp", axis=0, tiled=True),
        lax.all_gather(step_in, "fsdp", axis=0, tiled=True),
        lax.all_gather(attn_in, "fsdp", axis=0, tiled=True),
        lax.all_gather(mamba_out, "fsdp", axis=0, tiled=True),
        lax.all_gather(attn_out, "fsdp", axis=0, tiled=True),
        lax.all_gather(gate_up, "fsdp", axis=0, tiled=True),
        lax.all_gather(down_proj, "fsdp", axis=0, tiled=True),
    )
    first_gain = gathered[0].astype(fl_type)
    mixer_gain = gathered[1].astype(fl_type)
    second_gain = gathered[2].astype(fl_type)
    w_mamba_in, w_step_in, w_attn_in, w_mamba_out, w_attn_out, w_gate_up, w_down = gathered[3:]
    residual = hidden_in[0].astype(fl_type)
    first_scale = rms_scale(residual)
    first_norm = residual * first_scale
    normed = (first_norm * first_gain).astype(bf_type)
    projected = jnp.dot(normed, w_mamba_in, preferred_element_type=fl_type)
    gate_raw = projected[:, :DI]
    conv_in = projected[:, DI:].astype(bf_type)
    step_raw = jnp.dot(normed, w_step_in, preferred_element_type=fl_type).astype(bf_type)
    qkv_out = jnp.dot(normed, w_attn_in, preferred_element_type=fl_type).astype(bf_type)
    query_all = qkv_out[:, : QH * HD]
    key_part = qkv_out[:, QH * HD : (QH + KVH) * HD].reshape(block_rows, KVH, HD)
    value_part = qkv_out[:, (QH + KVH) * HD :].reshape(block_rows, KVH, HD)
    kv_pairs = jnp.concatenate([key_part, value_part], axis=2)
    kv_copies = kv_pairs[:, owners, :].reshape(block_rows, seq_count * 2 * HD)
    bc_copies = jnp.tile(conv_in[:, DI:], (1, seq_count))
    received = (
        lax.all_to_all(conv_in[:, :DI], "seq", split_axis=1, concat_axis=0, tiled=True),
        lax.all_to_all(bc_copies, "seq", split_axis=1, concat_axis=0, tiled=True),
        lax.all_to_all(step_raw, "seq", split_axis=1, concat_axis=0, tiled=True),
        lax.all_to_all(query_all, "seq", split_axis=1, concat_axis=0, tiled=True),
        lax.all_to_all(kv_copies, "seq", split_axis=1, concat_axis=0, tiled=True),
    )
    seg_ids = segments[0]
    taps = jnp.concatenate(
        [lax.dynamic_slice_in_dim(conv_taps, seq_index * x_width, x_width, 1), conv_taps[:, DI:]],
        axis=1,
    )
    tap_bias = jnp.concatenate(
        [lax.dynamic_slice_in_dim(conv_bias, seq_index * x_width, x_width, 0), conv_bias[DI:]]
    )
    params = (
        taps,
        tap_bias,
        lax.dynamic_slice_in_dim(step_bias, seq_index * head_share, head_share, 0),
        lax.dynamic_slice_in_dim(log_decay, seq_index * head_share, head_share, 0),
        lax.dynamic_slice_in_dim(skip_gain, seq_index * head_share, head_share, 0),
    )
    inputs = (
        received[0].astype(fl_type),
        received[1].astype(fl_type),
        received[2].astype(fl_type),
        received[3].astype(fl_type),
        received[4].astype(fl_type),
    )
    (ssm_group, attn_group), pull_back = jax.vjp(partial(core_apply, seg_ids), inputs, params)
    returned = (
        lax.all_to_all(ssm_group.astype(bf_type), "seq", split_axis=0, concat_axis=1, tiled=True),
        lax.all_to_all(attn_group.astype(bf_type), "seq", split_axis=0, concat_axis=1, tiled=True),
    )
    scan_out = returned[0]
    attn_mix = returned[1]
    scan_float = scan_out.astype(fl_type)
    gate_act = jax.nn.silu(gate_raw)
    gated = scan_float * gate_act
    gated_scale = rms_scale(gated)
    gated_norm = gated * gated_scale
    gated_b = (gated_norm * mixer_gain).astype(bf_type)
    mixed = (
        residual
        + jnp.dot(gated_b, w_mamba_out, preferred_element_type=fl_type)
        + jnp.dot(attn_mix, w_attn_out, preferred_element_type=fl_type)
    )
    second_scale = rms_scale(mixed)
    second_norm = mixed * second_scale
    ffn_in = (second_norm * second_gain).astype(bf_type)
    gate_vals = jnp.dot(ffn_in, w_gate_up, preferred_element_type=fl_type)
    gate_lin = gate_vals[:, :FF]
    up_lin = gate_vals[:, FF:]
    ffn_act = (jax.nn.silu(gate_lin) * up_lin).astype(bf_type)
    layer_out = (mixed + jnp.dot(ffn_act, w_down, preferred_element_type=fl_type)).astype(bf_type)
    first_gain_b = gathered[0].astype(fl_type)
    mixer_gain_b = gathered[1].astype(fl_type)
    second_gain_b = gathered[2].astype(fl_type)
    b_mamba_in, b_step_in, b_attn_in, b_mamba_out, b_attn_out, b_gate_up, b_down = gathered[3:]
    cot_in = grad_out[0]
    cot_float = cot_in.astype(fl_type)
    g_down = jnp.einsum("tf,td->fd", ffn_act, cot_in, preferred_element_type=fl_type)
    d_act = jnp.einsum("td,fd->tf", cot_in, b_down, preferred_element_type=fl_type)
    d_ffn = jnp.concatenate(
        [d_act * up_lin * swish_slope(gate_lin), d_act * jax.nn.silu(gate_lin)], axis=1
    ).astype(bf_type)
    g_gate_up = jnp.einsum("td,tf->df", ffn_in, d_ffn, preferred_element_type=fl_type)
    d_ffn_in = jnp.einsum("tf,df->td", d_ffn, b_gate_up, preferred_element_type=fl_type)
    g_ffn_gain = jnp.sum(d_ffn_in * second_norm, axis=0)
    ffn_shards = (
        lax.psum_scatter(g_ffn_gain, "fsdp", scatter_dimension=0, tiled=True),
        lax.psum_scatter(g_gate_up, "fsdp", scatter_dimension=0, tiled=True),
        lax.psum_scatter(g_down, "fsdp", scatter_dimension=0, tiled=True),
    )
    d_second = d_ffn_in * second_gain_b
    d_mixed = cot_float + second_scale * (
        d_second - second_norm * jnp.mean(d_second * second_norm, axis=-1, keepdims=True)
    )
    d_mixed_b = d_mixed.astype(bf_type)
    g_attn_out = jnp.einsum("tq,td->qd", attn_mix, d_mixed_b, preferred_element_type=fl_type)
    d_attn_mix = jnp.einsum(
        "td,qd->tq", d_mixed_b, b_attn_out, preferred_element_type=fl_type
    ).astype(bf_type)
    g_mamba_out = jnp.einsum("ti,td->id", gated_b, d_mixed_b, preferred_element_type=fl_type)
    d_gated_b = jnp.einsum("td,id->ti", d_mixed_b, b_mamba_out, preferred_element_type=fl_type)
    g_gated_gain = jnp.sum(d_gated_b * gated_norm, axis=0)
    d_gnorm = d_gated_b * mixer_gain_b
    d_gated = gated_scale * (
        d_gnorm - gated_norm * jnp.mean(d_gnorm * gated_norm, axis=-1, keepdims=True)
    )
    d_scan = (d_gated * gate_act).astype(bf_type)
    d_gate_raw = d_gated * scan_float * swish_slope(gate_raw)
    head_cots = (
        lax.all_to_all(d_scan, "seq", split_axis=1, concat_axis=0, tiled=True),
        lax.all_to_all(d_attn_mix, "seq", split_axis=1, concat_axis=0, tiled=True),
    )
    grad_inputs, grad_params = pull_back(
        (head_cots[0].astype(fl_type), head_cots[1].astype(fl_type))
    )
    tok_grads = (
        lax.all_to_all(
            grad_inputs[0].astype(bf_type), "seq", split_axis=0, concat_axis=1, tiled=True
        ),
        lax.all_to_all(
            grad_inputs[1].astype(bf_type), "seq", split_axis=0, concat_axis=1, tiled=True
        ),
        lax.all_to_all(
            grad_inputs[2].astype(bf_type), "seq", split_axis=0, concat_axis=1, tiled=True
        ),
        lax.all_to_all(
            grad_inputs[3].astype(bf_type), "seq", split_axis=0, concat_axis=1, tiled=True
        ),
        lax.all_to_all(
            grad_inputs[4].astype(bf_type), "seq", split_axis=0, concat_axis=1, tiled=True
        ),
    )
    bc_total = jnp.sum(tok_grads[1].astype(fl_type).reshape(block_rows, seq_count, 2 * NST), axis=1)
    kv_slots = tok_grads[4].astype(fl_type).reshape(block_rows, seq_count, 2 * HD)
    key_grads, value_grads = ([], [])
    for kv_head in range(KVH):
        users = [group for group in range(seq_count) if owners[group] == kv_head]
        head_total = kv_slots[:, users[0]]
        for group in users[1:]:
            head_total = head_total + kv_slots[:, group]
        key_grads.append(head_total[:, :HD])
        value_grads.append(head_total[:, HD:])
    d_proj = jnp.concatenate(
        [d_gate_raw.astype(bf_type), tok_grads[0], bc_total.astype(bf_type)], axis=1
    )
    d_step = tok_grads[2]
    d_qkv = jnp.concatenate(
        [
            tok_grads[3],
            jnp.concatenate(key_grads, axis=1).astype(bf_type),
            jnp.concatenate(value_grads, axis=1).astype(bf_type),
        ],
        axis=1,
    )
    g_mamba_in = jnp.einsum("td,tc->dc", normed, d_proj, preferred_element_type=fl_type)
    g_step_in = jnp.einsum("td,tc->dc", normed, d_step, preferred_element_type=fl_type)
    g_attn_in = jnp.einsum("td,tc->dc", normed, d_qkv, preferred_element_type=fl_type)
    d_normed = (
        jnp.einsum("tc,dc->td", d_proj, b_mamba_in, preferred_element_type=fl_type)
        + jnp.einsum("tc,dc->td", d_step, b_step_in, preferred_element_type=fl_type)
        + jnp.einsum("tc,dc->td", d_qkv, b_attn_in, preferred_element_type=fl_type)
    )
    g_norm_gain = jnp.sum(d_normed * first_norm, axis=0)
    d_first = d_normed * first_gain_b
    grad_tok = d_mixed + first_scale * (
        d_first - first_norm * jnp.mean(d_first * first_norm, axis=-1, keepdims=True)
    )
    mixer_shards = (
        lax.psum_scatter(g_norm_gain, "fsdp", scatter_dimension=0, tiled=True),
        lax.psum_scatter(g_gated_gain, "fsdp", scatter_dimension=0, tiled=True),
        lax.psum_scatter(g_mamba_in, "fsdp", scatter_dimension=0, tiled=True),
        lax.psum_scatter(g_step_in, "fsdp", scatter_dimension=0, tiled=True),
        lax.psum_scatter(g_attn_in, "fsdp", scatter_dimension=0, tiled=True),
        lax.psum_scatter(g_mamba_out, "fsdp", scatter_dimension=0, tiled=True),
        lax.psum_scatter(g_attn_out, "fsdp", scatter_dimension=0, tiled=True),
    )
    summed = (
        lax.psum(mixer_shards[0].astype(jnp.bfloat16), "seq").astype(jnp.float32),
        lax.psum(mixer_shards[1].astype(jnp.bfloat16), "seq").astype(jnp.float32),
        lax.psum(mixer_shards[2].astype(jnp.bfloat16), "seq").astype(jnp.float32),
        lax.psum(mixer_shards[3].astype(jnp.bfloat16), "seq").astype(jnp.float32),
        lax.psum(mixer_shards[4].astype(jnp.bfloat16), "seq").astype(jnp.float32),
        lax.psum(mixer_shards[5].astype(jnp.bfloat16), "seq").astype(jnp.float32),
        lax.psum(mixer_shards[6].astype(jnp.bfloat16), "seq").astype(jnp.float32),
        lax.psum(ffn_shards[0].astype(jnp.bfloat16), "seq").astype(jnp.float32),
        lax.psum(ffn_shards[1].astype(jnp.bfloat16), "seq").astype(jnp.float32),
        lax.psum(ffn_shards[2].astype(jnp.bfloat16), "seq").astype(jnp.float32),
    )
    zero_index = jnp.int32(0)
    taps_total = lax.dynamic_update_slice(
        jnp.zeros((KC, DI + 2 * NST), fl_type),
        grad_params[0][:, :x_width],
        (zero_index, seq_index * x_width),
    )
    taps_total = taps_total.at[:, DI:].set(grad_params[0][:, x_width:])
    bias_total = lax.dynamic_update_slice(
        jnp.zeros((DI + 2 * NST,), fl_type), grad_params[1][:x_width], (seq_index * x_width,)
    )
    bias_total = bias_total.at[DI:].set(grad_params[1][x_width:])
    step_total = lax.dynamic_update_slice(
        jnp.zeros((MH,), fl_type), grad_params[2], (seq_index * head_share,)
    )
    decay_total = lax.dynamic_update_slice(
        jnp.zeros((MH,), fl_type), grad_params[3], (seq_index * head_share,)
    )
    skip_total = lax.dynamic_update_slice(
        jnp.zeros((MH,), fl_type), grad_params[4], (seq_index * head_share,)
    )
    small = lax.psum((taps_total, bias_total, step_total, decay_total, skip_total), ("seq", "fsdp"))
    return (
        layer_out[None],
        grad_tok[None],
        summed[0],
        summed[2],
        summed[3],
        summed[4],
        small[0],
        small[1],
        small[2],
        small[3],
        small[4],
        summed[1],
        summed[5],
        summed[6],
        summed[7],
        summed[8],
        summed[9],
    )


def solution(mesh):
    placed = (
        P("fsdp", "seq", None),
        P("fsdp", "seq", None),
        P("fsdp", None),
        P("fsdp"),
        P("fsdp", None),
        P("fsdp", None),
        P("fsdp", None),
        P(),
        P(),
        P(),
        P(),
        P(),
        P("fsdp"),
        P("fsdp", None),
        P("fsdp", None),
        P("fsdp"),
        P("fsdp", None),
        P("fsdp", None),
    )
    return jax.shard_map(
        shards,
        mesh=mesh,
        in_specs=placed,
        out_specs=(
            P("fsdp", "seq", None),
            P("fsdp", "seq", None),
            P("fsdp"),
            P("fsdp", None),
            P("fsdp", None),
            P("fsdp", None),
            P(),
            P(),
            P(),
            P(),
            P(),
            P("fsdp"),
            P("fsdp", None),
            P("fsdp", None),
            P("fsdp"),
            P("fsdp", None),
            P("fsdp", None),
        ),
        check_vma=False,
    )
```

profile of v0, /device:TPU:0, one launch (start us, length us, event | category | flops | bytes accessed | tf_op | source)
XLA Modules:
  0.0 1727.9 jit_solution(10381162853957338975)
XLA Ops:
  10.7 22.3 %all-gather = bf16[8,1,128]{2,1,0:T(2,128)(2,1)S(1)} all-gather(bf16[1,1,128]{2,1,0:T(2,128)(2,1)S(1)} %bitcast.762), channel_id=1, replica_groups=mesh['seq'=4,'fsdp'=8] {'fsdp'}, dimensions={0}, use_global_device_ids=true | all-gather | bytes 2304 | tf_op jit(solution)/shard_map/all_gather | solution.py:194
  33.0 26.5 %all_gather.31 = bf16[1024,24]{0,1:T(8,128)(2,1)S(1)} all-gather(bf16[128,24]{0,1:T(8,128)(2,1)S(1)} %copy-done.105), channel_id=1, replica_groups=mesh['seq'=4,'fsdp'=8] {'fsdp'}, dimensions={0}, use_global_device_ids=true | all-gather | bytes 55296 | tf_op jit(solution)/shard_map/all_gather | solution.py:198
  70.5 18.2 %all-reduce.23 = bf16[1536]{0:T(1024)(128)(2,1)S(1)} all-reduce(bf16[1536]{0:T(1024)(128)(2,1)S(1)} %dynamic-update-slice.5), channel_id=1, replica_groups=mesh['seq'=4,'fsdp'=8] {'fsdp'}, use_global_device_ids=true, to_apply=%add.23 | all-reduce | flops 1536 | bytes 6144
  89.3 18.6 %all-gather.1 = bf16[8,1,128]{2,1,0:T(2,128)(2,1)S(1)} all-gather(bf16[1,1,128]{2,1,0:T(2,128)(2,1)S(1)} %bitcast.763), channel_id=1, replica_groups=mesh['seq'=4,'fsdp'=8] {'fsdp'}, dimensions={0}, use_global_device_ids=true | all-gather | bytes 2304 | tf_op jit(solution)/shard_map/all_gather | solution.py:196
  117.6 3.9 all-to-all-done.4
  125.8 3.6 all-to-all-done.5
  129.8 33.7 %all-gather.9.cloned.1.call-done = bf16[1024,3328]{1,0:T(8,128)(2,1)} async-done(((bf16[128,3328]{1,0:T(8,128)(2,1)}), bf16[1024,3328]{1,0:T(8,128)(2,1)}) %all-gather.9.cloned.1.call-update) | async-done | bytes 6815760 | tf_op jit(solution)/shard_map/all_gather | solution.py:197
  163.5 5.2 fusion.253
  173.7 5.1 all-to-all-done.2
  178.8 3.8 all-to-all-start.1
  183.0 4.1 fusion.254
  201.2 126.7 %while.82 = (s32[]{:T(128)}, f32[6,128,64]{1,2,0:T(8,128)S(1)}, s32[]{:T(128)}, f32[4,128,6,64]{1,0,3,2:T(4,128)}, f32[4,128,128]{1,2,0:T(8,128)}, /*index=5*/pr...) while((s32[]{:T(128)}, f32[6,128,64]{1,2,0:T(8,128)S(1)}, ...), condition=%wide.region_3.4_spmd.clone, body=%wide.region_1.3_spmd.clone.sunk | while | flops 252941824 | bytes 5576259 | solution.py:74
  214.8 6.0 dynamic_update_slice.277
  246.5 6.0 dynamic_update_slice.277
  278.2 6.0 dynamic_update_slice.277
  309.9 6.0 dynamic_update_slice.277
  341.7 4.1 all-to-all-done.3
  345.8 3.8 all-to-all-start.6
  352.2 3.6 convolution_add_fusion.4
  357.7 32.4 %all-gather.17.cloned.1.call-done = bf16[1024,4096]{1,0:T(8,128)(2,1)} async-done(((bf16[128,4096]{1,0:T(8,128)(2,1)}), bf16[1024,4096]{1,0:T(8,128)(2,1)}) %all-gather.17.cloned.1.call-update) | async-done | bytes 8388624 | tf_op jit(solution)/shard_map/all_gather | solution.py:202
  390.1 6.1 fusion.230
  396.2 66.8 %all-gather.19.cloned.1.call-done = bf16[2048,1024]{1,0:T(8,128)(2,1)} async-done(((bf16[256,1024]{1,0:T(8,128)(2,1)}), bf16[2048,1024]{1,0:T(8,128)(2,1)}) %all-gather.19.cloned.1.call-update) | async-done | bytes 4194320 | tf_op jit(solution)/shard_map/all_gather | solution.py:203
  463.0 5.4 multiply_convert_fusion.1
  478.2 4.3 all-to-all-start.7
  482.5 7.4 all-to-all-done.7
  495.6 144.1 %while.83 = (s32[]{:T(128)}, f32[6,128,64]{1,2,0:T(8,128)S(1)}, f32[4,128,6,64]{1,0,3,2:T(4,128)}, f32[4,128,128]{2,1,0:T(8,128)}, f32[4,128,128]{2,1,0:T(8,128)...) while((s32[]{:T(128)}, f32[6,128,64]{1,2,0:T(8,128)S(1)}, ...), condition=%wide.region_19.20_spmd.clone, body=%wide.region_10.19_spmd.clone.sunk | while | flops 505208320 | bytes 8949151 | solution.py:74
  516.7 6.0 dynamic_update_slice.283
  552.7 6.0 dynamic_update_slice.283
  588.8 6.0 dynamic_update_slice.283
  624.8 6.0 dynamic_update_slice.283
  677.1 4.0 all-to-all-done.12
  685.3 3.6 fusion.231
  690.0 4.5 fusion.181
  712.8 5.2 all-to-all-done.9
  721.5 7.3 all-to-all-done.8
  728.9 6.9 fusion.176
  737.0 8.3 fusion.158
  746.9 3.6 fusion.139
  751.8 40.4 %all-reduce.27 = (f32[4,1792]{1,0:T(4,128)}, f32[1792]{0:T(1024)}, f32[24]{0:T(128)}, f32[24]{0:T(128)}, f32[24]{0:T(128)}) all-reduce(f32[4,1792]{1,0:T(4,128)S(1)} %add_dynamic-update-slice_fusion, f32[1792]{0:T(1024)S(1)} %slice_dynamic-update-slice_fusion.1, ...), channel_id=1, replica_groups=mesh['seq'=4,'fsdp'=8] {'seq','fsdp'}, use_global_device_ids=true, to_apply=%region_36.37 | all-reduce | flops 9032 | bytes 72256 | tf_op jit(solution)/shard_map/psum | solution.py:416
  794.6 67.8 %reduce-scatter.12.cloned.1.call-done = f32[128,768]{1,0:T(8,128)} async-done(((f32[1024,768]{1,0:T(8,128)}), f32[128,768]{1,0:T(8,128)}) %reduce-scatter.12.cloned.1.call-update) | async-done | bytes 393232 | tf_op jit(solution)/shard_map/reduce_scatter | solution.py:380
  864.1 118.9 %reduce-scatter.14.cloned.1.call-done = f32[192,1024]{1,0:T(8,128)} async-done(((f32[1536,1024]{1,0:T(8,128)}), f32[192,1024]{1,0:T(8,128)}) %reduce-scatter.14.cloned.1.call-update) | async-done | bytes 786448 | tf_op jit(solution)/shard_map/reduce_scatter | solution.py:381
  985.0 148.5 %reduce-scatter.20.cloned.1.call-done = f32[256,1024]{1,0:T(8,128)} async-done(((f32[2048,1024]{1,0:T(8,128)}), f32[256,1024]{1,0:T(8,128)}) %reduce-scatter.20.cloned.1.call-update) | async-done | bytes 1048592 | tf_op jit(solution)/shard_map/reduce_scatter | solution.py:296
  1135.5 222.6 %reduce-scatter.8.cloned.1.call-done = f32[128,3328]{1,0:T(8,128)} async-done(((f32[1024,3328]{1,0:T(8,128)}), f32[128,3328]{1,0:T(8,128)}) %reduce-scatter.8.cloned.1.call-update) | async-done | bytes 1703952 | tf_op jit(solution)/shard_map/reduce_scatter | solution.py:378
  1360.5 280.6 %reduce-scatter.18.cloned.1.call-done = f32[128,4096]{1,0:T(8,128)} async-done(((f32[1024,4096]{1,0:T(8,128)}), f32[128,4096]{1,0:T(8,128)}) %reduce-scatter.18.cloned.1.call-update) | async-done | bytes 2097168 | tf_op jit(solution)/shard_map/reduce_scatter | solution.py:295
  1643.9 5.3 fusion.177
  1650.4 35.2 %all-reduce.28 = (bf16[1024]{0:T(1024)(128)(2,1)S(1)}, bf16[1536]{0:T(1024)(128)(2,1)S(1)}, bf16[1024]{0:T(1024)(128)(2,1)S(1)}) all-reduce(f32[1024]{0:T(1024)S(1)} %get-tuple-element.1514, f32[1536]{0:T(1024)S(1)} %copy-done.92, f32[1024]{0:T(1024)S(1)} %copy-done.101), channel_id=2, replica_groups=mesh['seq'=4,'fsdp'=8] {'fsdp'}, use_global_device_ids=true, to_apply=%region_24.25.clone | all-reduce | flops 3584 | bytes 21504
  1685.9 6.7 all-reduce.29
  1695.9 17.5 %all-reduce.33.cloned.1.call-done = (bf16[128,3328]{1,0:T(8,128)(2,1)}, bf16[128,768]{1,0:T(8,128)(2,1)}, bf16[192,1024]{1,0:T(8,128)(2,1)}, bf16[64,1024]{1,0:T...) async-done(((bf16[128,3328]{1,0:T(8,128)(2,1)}, bf16[128,768]{1,0:T(8,128)(2,1)}, bf16[192,1024]{1,0:T(8,128)(2,1)}, bf16[64,1024]{1,0:T(8,128)(2,1)}, ...) | async-done | bytes 3145744 | tf_op jit(solution)/shard_map/psum | solution.py:387
  (829 shorter events, 390.0 us)
Async XLA Ops:
  7.2 102.7 %all-gather.13.cloned.1.call-start = ((), (), s32[]{:S(2)}) async-start(), calls=%async_computation.23 | async-start | bytes 1769472 | tf_op jit(solution)/shard_map/all_gather | solution.py:199
  8.0 155.5 %all-gather.9.cloned.1.call-start = ((), (), s32[]{:S(2)}) async-start(), calls=%async_computation.21 | async-start | bytes 7667712 | tf_op jit(solution)/shard_map/all_gather | solution.py:197
  8.7 343.5 %all-gather.11.cloned.1.call-start = ((), (), s32[]{:S(2)}) async-start(), calls=%async_computation.22 | async-start | bytes 3538944 | tf_op jit(solution)/shard_map/all_gather | solution.py:200
  9.5 60.7 %copy-start.127 = (bf16[192]{0:T(256)(128)(2,1)S(1)}, bf16[192]{0:T(256)(128)(2,1)}, u32[]{:S(2)}) copy-start(bf16[192]{0:T(256)(128)(2,1)} %param.39) | copy-start | bytes 1156
  9.5 79.8 %copy-start.122 = (s32[4]{0:T(128)S(1)}, s32[4]{0:T(128)}, u32[]{:S(2)}) copy-start(s32[4]{0:T(128)} %constant.353) | copy-start | bytes 52
  9.5 79.8 %copy-start.121 = (bf16[128]{0:T(256)(128)(2,1)S(1)}, bf16[128]{0:T(256)(128)(2,1)}, u32[]{:S(2)}) copy-start(bf16[128]{0:T(256)(128)(2,1)} %param.42) | copy-start | bytes 772
  9.5 99.0 %slice-start = ((f32[4,1792]{1,0:T(4,128)}), f32[4,256]{1,0:T(4,128)S(1)}, s32[]{:S(2)}) async-start(f32[4,1792]{1,0:T(4,128)} %param.34), calls=%async_computation.35 | async-start | bytes 8192 | tf_op jit(solution)/shard_map/slice | solution.py:233
  9.5 346.3 %all-gather.15.cloned.1.call-start = ((), (), s32[]{:S(2)}) async-start(), calls=%async_computation.24 | async-start | bytes 1179648 | tf_op jit(solution)/shard_map/all_gather | solution.py:201
  10.1 380.0 %all-gather.17.cloned.1.call-start = ((), (), s32[]{:S(2)}) async-start(), calls=%async_computation.25 | async-start | bytes 9437184 | tf_op jit(solution)/shard_map/all_gather | solution.py:202
  33.0 130.4 %copy-start.50 = (f32[8,1,128]{2,1,0:T(1,128)}, f32[8,1,128]{2,1,0:T(1,128)S(1)}, u32[]{:S(2)}) copy-start(f32[8,1,128]{2,1,0:T(1,128)S(1)} %convert_element_type.332) | copy-start | bytes 12292
  59.7 103.8 %copy-start.93 = (f32[128]{0:T(128)}, f32[128]{0:T(128)S(1)}, u32[]{:S(2)}) copy-start(f32[128]{0:T(128)S(1)} %add_rsqrt_fusion.2) | copy-start | bytes 1540
  60.6 53.0 %all-to-all-start = ((bf16[128,4,6]{0,2,1:T(8,128)(2,1)}), bf16[128,4,6]{0,2,1:T(8,128)(2,1)S(1)}, u32[]{:S(2)}, u32[]{:S(2)}) async-start(bf16[128,4,6]{0,2,1:T(8,128)(2,1)} %all_to_all.148), calls=%async_computation | async-start | bytes 16384 | tf_op jit(solution)/shard_map/all_to_all | solution.py:227
  63.8 399.2 %all-gather.19.cloned.1.call-start = ((), (), s32[]{:S(2)}) async-start(), calls=%async_computation.26 | async-start | bytes 4718592 | tf_op jit(solution)/shard_map/all_gather | solution.py:203
  66.1 116.5 %copy-start.106 = (f32[32]{0:T(128)}, f32[32]{0:T(128)S(1)}, u32[]{:S(2)}) copy-start(f32[32]{0:T(128)S(1)} %multiply_exponential_fusion) | copy-start | bytes 388
  68.0 115.0 %copy-start.43 = (pred[512,512]{0,1:T(8,128)(4,1)}, pred[512,512]{0,1:T(8,128)(4,1)S(1)}, u32[]{:S(2)}) copy-start(pred[512,512]{0,1:T(8,128)(4,1)S(1)} %fusion.154) | copy-start | bytes 786436
  89.3 93.3 %copy-start.90 = (f32[512]{0:T(512)}, f32[512]{0:T(512)S(1)}, u32[]{:S(2)}) copy-start(f32[512]{0:T(512)S(1)} %add_convert_fusion.4) | copy-start | bytes 6148
  108.5 81.5 %copy-start.80 = (f32[640]{0:T(1024)}, f32[640]{0:T(1024)S(1)}, u32[]{:S(2)}) copy-start(f32[640]{0:T(1024)S(1)} %get-tuple-element.1516) | copy-start | bytes 7684
  108.5 81.5 %copy-start.82 = (f32[640]{0:T(1024)}, f32[640]{0:T(1024)S(1)}, u32[]{:S(2)}) copy-start(f32[640]{0:T(1024)S(1)} %get-tuple-element.1517) | copy-start | bytes 7684
  108.6 81.5 %copy-start.84 = (f32[640]{0:T(1024)}, f32[640]{0:T(1024)S(1)}, u32[]{:S(2)}) copy-start(f32[640]{0:T(1024)S(1)} %get-tuple-element.1518) | copy-start | bytes 7684
  108.6 81.5 %copy-start.86 = (f32[640]{0:T(1024)}, f32[640]{0:T(1024)S(1)}, u32[]{:S(2)}) copy-start(f32[640]{0:T(1024)S(1)} %get-tuple-element.1519) | copy-start | bytes 7684
  109.8 80.2 %copy-start.108 = (pred[512]{0:T(512)(128)(4,1)}, pred[512]{0:T(512)(128)(4,1)S(1)}, u32[]{:S(2)}) copy-start(pred[512]{0:T(512)(128)(4,1)S(1)} %get-tuple-element.1725) | copy-start | bytes 1540
  109.8 80.3 %copy-start.110 = (pred[512]{0:T(512)(128)(4,1)}, pred[512]{0:T(512)(128)(4,1)S(1)}, u32[]{:S(2)}) copy-start(pred[512]{0:T(512)(128)(4,1)S(1)} %get-tuple-element.1726) | copy-start | bytes 1540
  109.8 80.3 %copy-start.112 = (pred[512]{0:T(512)(128)(4,1)}, pred[512]{0:T(512)(128)(4,1)S(1)}, u32[]{:S(2)}) copy-start(pred[512]{0:T(512)(128)(4,1)S(1)} %get-tuple-element.1727) | copy-start | bytes 1540
  113.6 7.9 all-to-all-start.4
  121.5 7.9 all-to-all-start.5
  169.4 9.4 all-to-all-start.2
  178.8 11.1 all-to-all-start.1
  335.0 10.8 all-to-all-start.3
  345.8 10.0 all-to-all-start.6
  352.2 122.7 %copy-start.1 = (f32[128,1536]{1,0:T(8,128)}, f32[128,1536]{1,0:T(8,128)S(1)}, u32[]{:S(2)}) copy-start(f32[128,1536]{1,0:T(8,128)S(1)} %get-tuple-element.1670) | copy-start | bytes 2359300
  352.2 120.8 %copy-start.103 = (f32[128]{0:T(128)}, f32[128]{0:T(128)S(1)}, u32[]{:S(2)}) copy-start(f32[128]{0:T(128)S(1)} %add_rsqrt_fusion.1) | copy-start | bytes 1540
  357.7 114.3 %copy-start.88 = (f32[128]{0:T(128)}, f32[128]{0:T(128)S(1)}, u32[]{:S(2)}) copy-start(f32[128]{0:T(128)S(1)} %add_rsqrt_fusion) | copy-start | bytes 1540
  390.1 72.9 %copy-start.30 = (bf16[1,128,1024]{2,1,0:T(8,128)(2,1)S(1)}, bf16[1,128,1024]{2,1,0:T(8,128)(2,1)}, u32[]{:S(2)}) copy-start(bf16[1,128,1024]{2,1,0:T(8,128)(2,1)} %param.28) | copy-start | bytes 786436
  478.2 11.8 all-to-all-start.7
  641.9 7.0 all-to-all-start.10
  648.9 7.9 all-to-all-start.11
  652.3 140.0 %reduce-scatter.10.cloned.1.call-start = ((), (), s32[]{:S(2)}) async-start(), calls=%async_computation.28 | async-start | bytes 110592 | tf_op jit(solution)/shard_map/reduce_scatter | solution.py:379
  653.3 139.7 %reduce-scatter.16.cloned.1.call-start = ((), (), s32[]{:S(2)}) async-start(), calls=%async_computation.31 | async-start | bytes 2359296 | tf_op jit(solution)/shard_map/reduce_scatter | solution.py:382
  665.0 8.1 all-to-all-start.13
  673.1 7.9 all-to-all-start.12
  676.5 186.0 %reduce-scatter.12.cloned.1.call-start = ((), (), s32[]{:S(2)}) async-start(), calls=%async_computation.29 | async-start | bytes 3538944 | tf_op jit(solution)/shard_map/reduce_scatter | solution.py:380
  684.2 298.9 %reduce-scatter.14.cloned.1.call-start = ((), (), s32[]{:S(2)}) async-start(), calls=%async_computation.30 | async-start | bytes 7077888 | tf_op jit(solution)/shard_map/reduce_scatter | solution.py:381
  688.9 444.5 %reduce-scatter.20.cloned.1.call-start = ((), (), s32[]{:S(2)}) async-start(), calls=%async_computation.33 | async-start | bytes 9437184 | tf_op jit(solution)/shard_map/reduce_scatter | solution.py:296
  708.4 9.5 all-to-all-start.9
  718.0 10.8 all-to-all-start.8
  721.4 636.7 %reduce-scatter.8.cloned.1.call-start = ((), (), s32[]{:S(2)}) async-start(), calls=%async_computation.27 | async-start | bytes 15335424 | tf_op jit(solution)/shard_map/reduce_scatter | solution.py:378
  735.8 905.3 %reduce-scatter.18.cloned.1.call-start = ((), (), s32[]{:S(2)}) async-start(), calls=%async_computation.32 | async-start | bytes 18874368 | tf_op jit(solution)/shard_map/reduce_scatter | solution.py:295
  745.3 968.1 %all-reduce.33.cloned.1.call-start = ((), (), s32[]{:S(2)}) async-start(), calls=%async_computation.34 | async-start | bytes 6291456 | tf_op jit(solution)/shard_map/psum | solution.py:387
  (133 other events, 1477.4 us)
Sparse Core Ops, SparseCore 0:
  10.2 47.0 all-gather.12
  59.5 103.9 all-gather.8
  165.7 58.2 all-gather.10
  225.9 38.9 all-gather.14
  266.8 123.2 all-gather.16
  392.1 70.8 all-gather.18
  656.3 58.1 reduce-scatter.9
  718.0 67.7 reduce-scatter.15
  789.4 72.9 reduce-scatter.11
  865.9 117.1 reduce-scatter.13
  986.7 146.7 reduce-scatter.19
  1136.9 221.1 reduce-scatter.7
  1361.9 279.2 reduce-scatter.17
  1645.5 67.8 all-reduce.32
where the time goes:
time: 1740 us; the launch traced here: 1730 us
  waiting for transfers between devices  1040 us (60%)
  local copies, waits for them, and re-layouts  179 us (10%)
  blocking collectives  168 us (10%)
  matrix products  156 us (9%)
  other arithmetic  112 us (6%)
  starting transfers between devices  49.9 us (3%)
  between operations  18.1 us (1%)
    reduce_scatter x1, waiting for transfers between devices, shards(): lax.psum_scatter(g_gate_up, 'fsdp', scatter_dimension=0, tiled=True)  281 us
    reduce_scatter x1, waiting for transfers between devices, shards(): lax.psum_scatter(g_mamba_in, 'fsdp', scatter_dimension=0, tiled=True)  223 us
    reduce_scatter x1, waiting for transfers between devices, shards(): lax.psum_scatter(g_down, 'fsdp', scatter_dimension=0, tiled=True)  148 us
    reduce_scatter x1, waiting for transfers between devices, shards(): lax.psum_scatter(g_mamba_out, 'fsdp', scatter_dimension=0, tiled=True)  119 us
    dynamic_update_slice x68, local copies, waits for them, and re-layouts, scan_blocks(): final, outputs = lax.scan(one_block, start, items)  82.6 us
    reduce_scatter x1, waiting for transfers between devices, shards(): lax.psum_scatter(g_attn_in, 'fsdp', scatter_dimension=0, tiled=True)  67.8 us
    all_gather x1, waiting for transfers between devices, shards(): lax.all_gather(down_proj, 'fsdp', axis=0, tiled=True)  66.8 us
    unnamed x2, blocking collectives  53.4 us
  transfers between devices with their start and end apart: 28, of which 21 were waited for; matrix products, arithmetic and copies ran while one was open for 15% of the time, Pallas kernels for 0%

commit v1 on v0

v1 whole, which is shorter than its diff:
```python
from functools import partial
import math

import jax
import jax.numpy as jnp
from jax import lax
from jax.sharding import PartitionSpec as P

MH = 24
HD = 64
NST = 128
KC = 4
QH = 8
KVH = 2
FF = 2048
DI = 1536


EPS = 1e-05
ROPE_THETA = 10000.0


def rms_scale(values):
    return lax.rsqrt(jnp.mean(values * values, axis=-1, keepdims=True) + EPS)


def swish_slope(values):
    sigma = jax.nn.sigmoid(values)
    return sigma * (1.0 + values * (1.0 - sigma))


def seq_gather(array):
    return lax.all_gather(array, "seq", axis=0, tiled=True)


def seq_exchange(blocks):
    return lax.all_to_all(blocks, "seq", split_axis=0, concat_axis=0, tiled=True)


def seq_reduce(partial_sums):
    seq_count = lax.axis_size("seq")
    blocks = partial_sums.reshape(seq_count, -1, partial_sums.shape[1])
    return jnp.sum(seq_exchange(blocks).astype(jnp.float32), axis=0)


def two_terms(column):
    high = column.astype(jnp.bfloat16)
    low = (column - high.astype(jnp.float32)).astype(jnp.bfloat16)
    return jnp.concatenate(
        [high, low, jnp.zeros((column.shape[0], 126), jnp.bfloat16)], axis=1
    )


def from_terms(terms):
    return terms[:, :1] + terms[:, 1:2]


def core_inputs(seg_ids, inputs, params):
    pre_conv, step_raw, query_in, key_in = inputs
    taps, tap_bias, step_bias, log_decay = params
    row_count = pre_conv.shape[0]
    tap_count = taps.shape[0]
    accum = tap_bias[None, :] + taps[tap_count - 1][None, :] * pre_conv
    for lag_step in range(1, tap_count):
        moved = jnp.concatenate(
            [
                jnp.zeros((lag_step, pre_conv.shape[1]), pre_conv.dtype),
                pre_conv[: row_count - lag_step],
            ],
            axis=0,
        )
        prior = jnp.concatenate(
            [jnp.full((lag_step,), -1, jnp.int32), seg_ids[: row_count - lag_step]]
        )
        same_seq = (prior == seg_ids)[:, None]
        accum = accum + taps[tap_count - 1 - lag_step][None, :] * jnp.where(same_seq, moved, 0.0)
    activated = jax.nn.silu(accum)
    step = jax.nn.softplus(step_raw + step_bias[None, :])
    log_step = -jnp.exp(log_decay)[None, :] * step
    positions = jnp.arange(row_count, dtype=jnp.int32)
    first_count = jnp.sum((seg_ids == 0).astype(jnp.int32))
    place = (positions - jnp.where(seg_ids == 0, 0, first_count)).astype(jnp.float32)
    half = HD // 2
    freqs = jnp.exp(-math.log(ROPE_THETA) * 2.0 * jnp.arange(half, dtype=jnp.float32) / HD)
    angles = place[:, None] * freqs[None, :]
    cosine = jnp.cos(angles)[:, None, :]
    sine = jnp.sin(angles)[:, None, :]

    def rotate(tensor):
        heads = tensor.reshape(row_count, -1, HD)
        first_half = heads[..., :half]
        second_half = heads[..., half:]
        return jnp.concatenate(
            [first_half * cosine - second_half * sine, second_half * cosine + first_half * sine],
            axis=-1,
        ).reshape(tensor.shape)

    return activated, step, log_step, rotate(query_in), rotate(key_in)


def shards(
    hidden_in,
    grad_out,
    segments,
    norm_gain,
    mamba_in,
    step_in,
    attn_in,
    conv_taps,
    conv_bias,
    step_bias,
    log_decay,
    skip_gain,
    gated_gain,
    mamba_out,
    attn_out,
    ffn_gain,
    gate_up,
    down_proj,
):
    bf_type = jnp.bfloat16
    fl_type = jnp.float32
    seq_count = lax.axis_size("seq")
    seq_index = lax.axis_index("seq")
    fsdp_count = lax.axis_size("fsdp")
    block_rows = hidden_in.shape[1]
    model = hidden_in.shape[2]
    rows = block_rows * seq_count
    own_rows = model // fsdp_count
    x_width = DI // seq_count
    head_share = MH // seq_count
    query_width = QH * HD // seq_count
    query_share = QH // seq_count
    ff_width = FF // seq_count
    col_width = model // seq_count
    owners = [group * KVH // seq_count for group in range(seq_count)]
    owner = seq_index * KVH // seq_count
    gain_own = DI // fsdp_count
    gain_cols = -(-gain_own // own_rows)

    def cols(array, start, size):
        return lax.dynamic_slice_in_dim(array, start, size, 1)

    gain_pad = jnp.pad(gated_gain, (0, gain_cols * own_rows - gain_own))
    in_parts = [
        cols(mamba_in, seq_index * x_width, x_width),
        cols(mamba_in, DI + seq_index * x_width, x_width),
        mamba_in[:, 2 * DI :],
        cols(attn_in, seq_index * query_width, query_width),
        cols(attn_in, QH * HD + owner * HD, HD),
        cols(attn_in, (QH + KVH) * HD + owner * HD, HD),
        cols(step_in, seq_index * head_share, head_share),
        norm_gain[:, None],
        ffn_gain[:, None],
        gain_pad.reshape(gain_cols, own_rows).T,
    ]
    main_width = 2 * x_width + 2 * NST + query_width + 2 * HD
    pad_width = 128 - head_share - 2 - gain_cols
    in_pack = jnp.concatenate(in_parts + [jnp.zeros((own_rows, pad_width), bf_type)], axis=1)
    out_cols = jnp.concatenate(
        [
            cols(mamba_out, seq_index * col_width, col_width),
            cols(attn_out, seq_index * col_width, col_width),
            cols(down_proj, seq_index * col_width, col_width),
        ],
        axis=0,
    )
    chunks = out_cols.shape[0] // own_rows
    big_pack = jnp.concatenate(
        [
            cols(gate_up, seq_index * ff_width, ff_width),
            cols(gate_up, FF + seq_index * ff_width, ff_width),
        ]
        + [out_cols[at * own_rows : (at + 1) * own_rows] for at in range(chunks)],
        axis=1,
    )
    hidden_all = seq_gather(hidden_in[0])
    in_all = lax.all_gather(in_pack, "fsdp", axis=0, tiled=True)
    big_all = lax.all_gather(big_pack, "fsdp", axis=0, tiled=True)
    cot_all = seq_gather(grad_out[0])
    gain_at = main_width + head_share
    first_gain = in_all[:, gain_at].astype(fl_type)
    second_gain = in_all[:, gain_at + 1].astype(fl_type)
    gated_gains = (
        in_all[:, gain_at + 2 : gain_at + 2 + gain_cols]
        .reshape(fsdp_count, own_rows, gain_cols)
        .transpose(0, 2, 1)
        .reshape(fsdp_count, gain_cols * own_rows)[:, :gain_own]
        .reshape(DI)
    )
    mixer_gain = lax.dynamic_slice_in_dim(gated_gains, seq_index * x_width, x_width, 0).astype(
        fl_type
    )
    w_gate_up = big_all[:, : 2 * ff_width]
    out_all = (
        big_all[:, 2 * ff_width :]
        .reshape(fsdp_count, own_rows, chunks, col_width)
        .transpose(0, 2, 1, 3)
        .reshape(fsdp_count, chunks * own_rows, col_width)
    )
    attn_own = QH * HD // fsdp_count
    out_send = jnp.concatenate(
        [
            out_all[:, :gain_own].reshape(seq_count, x_width, col_width),
            out_all[:, gain_own : gain_own + attn_own].reshape(seq_count, query_width, col_width),
            out_all[:, gain_own + attn_own :].reshape(seq_count, ff_width, col_width),
        ],
        axis=1,
    )
    out_w = seq_exchange(out_send).transpose(1, 0, 2).reshape(x_width + query_width + ff_width, model)
    w_mamba_out = out_w[:x_width]
    w_attn_out = out_w[x_width : x_width + query_width]
    w_down = out_w[x_width + query_width :]

    res_all = hidden_all.astype(fl_type)
    normed = (res_all * rms_scale(res_all) * first_gain).astype(bf_type)
    projected = jnp.dot(normed, in_all, preferred_element_type=fl_type)
    gate_raw = projected[:, :x_width]
    inputs_b = projected[:, x_width:].astype(bf_type).astype(fl_type)
    conv_width = x_width + 2 * NST
    conv_in = inputs_b[:, :conv_width]
    query_in = inputs_b[:, conv_width : conv_width + query_width]
    key_in = inputs_b[:, conv_width + query_width : conv_width + query_width + HD]
    value_b = inputs_b[:, conv_width + query_width + HD : conv_width + query_width + 2 * HD].astype(
        bf_type
    )
    step_at = conv_width + query_width + 2 * HD
    step_raw = inputs_b[:, step_at : step_at + head_share]
    seg_ids = segments[0]
    taps = jnp.concatenate(
        [cols(conv_taps, seq_index * x_width, x_width), conv_taps[:, DI:]], axis=1
    )
    tap_bias = jnp.concatenate(
        [lax.dynamic_slice_in_dim(conv_bias, seq_index * x_width, x_width, 0), conv_bias[DI:]]
    )
    params = (
        taps,
        tap_bias,
        lax.dynamic_slice_in_dim(step_bias, seq_index * head_share, head_share, 0),
        lax.dynamic_slice_in_dim(log_decay, seq_index * head_share, head_share, 0),
    )
    skip = lax.dynamic_slice_in_dim(skip_gain, seq_index * head_share, head_share, 0)
    (activated, step, log_step, queries, keys), pull_back = jax.vjp(
        partial(core_inputs, seg_ids), (conv_in, step_raw, query_in, key_in), params
    )
    positions = jnp.arange(rows, dtype=jnp.int32)
    causal = positions[:, None] >= positions[None, :]
    mask = causal & (seg_ids[:, None] == seg_ids[None, :])
    highest = lax.Precision.HIGHEST
    x_all = activated[:, :x_width]
    b_mat = activated[:, x_width : x_width + NST].astype(bf_type)
    c_mat = activated[:, x_width + NST :].astype(bf_type)
    x_heads = x_all.reshape(rows, head_share, HD).transpose(1, 0, 2)
    step_t = step.T
    cum_t = jnp.dot(log_step.T, causal.T.astype(fl_type), precision=highest)
    inner = jnp.einsum("tn,pn->tp", c_mat, b_mat, preferred_element_type=fl_type)
    decay = jnp.exp(jnp.where(mask[None], cum_t[:, :, None] - cum_t[:, None, :], -1e30))
    kernel_b = (inner[None] * decay).astype(bf_type)
    x_step = (x_heads * step_t[:, :, None]).astype(bf_type)
    scan_y = jnp.einsum("htp,hpd->htd", kernel_b, x_step, preferred_element_type=fl_type)
    ssm = scan_y + skip[:, None, None] * x_heads
    scan_float = (
        ssm.astype(bf_type).transpose(1, 0, 2).reshape(rows, x_width).astype(fl_type)
    )
    key_b = keys.astype(bf_type)
    q_heads = queries.reshape(rows, query_share, HD).transpose(1, 0, 2)
    scores = jnp.einsum("hid,jd->hij", q_heads, keys, precision=highest) * (1.0 / math.sqrt(HD))
    weights = jnp.exp(jnp.where(mask[None], scores, -1e30))
    weights = weights / jnp.sum(weights, axis=-1, keepdims=True)
    weights_b = weights.astype(bf_type)
    attended = jnp.einsum("hij,jd->hid", weights_b, value_b, preferred_element_type=fl_type)
    attn_mix = attended.astype(bf_type).transpose(1, 0, 2).reshape(rows, query_width)

    gate_act = jax.nn.silu(gate_raw)
    gated = scan_float * gate_act
    square_part = jnp.sum(gated * gated, axis=-1, keepdims=True)
    gated_un = (gated * mixer_gain).astype(bf_type)
    mix_parts = jnp.concatenate(
        [
            jnp.dot(gated_un, w_mamba_out, preferred_element_type=fl_type).astype(bf_type),
            jnp.dot(attn_mix, w_attn_out, preferred_element_type=fl_type).astype(bf_type),
            two_terms(square_part),
        ],
        axis=1,
    )
    mix_sum = seq_reduce(mix_parts)
    residual = hidden_in[0].astype(fl_type)
    gated_scale = lax.rsqrt(from_terms(mix_sum[:, 2 * model :]) / DI + EPS)
    mamba_part = gated_scale * mix_sum[:, :model]
    mixed = residual + mamba_part + mix_sum[:, model : 2 * model]
    second_scale = rms_scale(mixed)
    second_norm = mixed * second_scale
    ffn_own = (second_norm * second_gain).astype(bf_type)
    ffn_got = seq_gather(jnp.concatenate([ffn_own, two_terms(gated_scale)], axis=1))
    ffn_in = ffn_got[:, :model]
    scale_all = from_terms(ffn_got[:, model:].astype(fl_type))
    gate_vals = jnp.dot(ffn_in, w_gate_up, preferred_element_type=fl_type)
    gate_lin = gate_vals[:, :ff_width]
    up_lin = gate_vals[:, ff_width:]
    ffn_act = (jax.nn.silu(gate_lin) * up_lin).astype(bf_type)
    d_act = jnp.einsum("td,fd->tf", cot_all, w_down, preferred_element_type=fl_type)
    d_ffn = jnp.concatenate(
        [d_act * up_lin * swish_slope(gate_lin), d_act * jax.nn.silu(gate_lin)], axis=1
    ).astype(bf_type)
    ffn_sum = seq_reduce(
        jnp.concatenate(
            [
                jnp.dot(ffn_act, w_down, preferred_element_type=fl_type).astype(bf_type),
                jnp.einsum("tf,df->td", d_ffn, w_gate_up, preferred_element_type=fl_type).astype(
                    bf_type
                ),
            ],
            axis=1,
        )
    )
    layer_out = (mixed + ffn_sum[:, :model]).astype(bf_type)
    d_ffn_in = ffn_sum[:, model:]
    g_down = jnp.einsum("tf,td->fd", ffn_act, cot_all, preferred_element_type=fl_type)
    g_gate_up = jnp.einsum("td,tf->df", ffn_in, d_ffn, preferred_element_type=fl_type)
    g_ffn_gain = jnp.sum(d_ffn_in * second_norm, axis=0)
    d_second = d_ffn_in * second_gain
    d_mixed = grad_out[0].astype(fl_type) + second_scale * (
        d_second - second_norm * jnp.mean(d_second * second_norm, axis=-1, keepdims=True)
    )
    d_mixed_own = d_mixed.astype(bf_type)
    mean_own = jnp.sum(d_mixed_own.astype(fl_type) * mamba_part, axis=-1, keepdims=True) / DI
    mixed_got = seq_gather(jnp.concatenate([d_mixed_own, two_terms(mean_own)], axis=1))
    d_mixed_b = mixed_got[:, :model]
    mean_all = from_terms(mixed_got[:, model:].astype(fl_type))
    gated_norm = gated * scale_all
    gated_b = (gated_norm * mixer_gain).astype(bf_type)
    g_attn_out = jnp.einsum("tq,td->qd", attn_mix, d_mixed_b, preferred_element_type=fl_type)
    g_mamba_out = jnp.einsum("ti,td->id", gated_b, d_mixed_b, preferred_element_type=fl_type)
    d_attn = jnp.einsum("td,qd->tq", d_mixed_b, w_attn_out, preferred_element_type=fl_type)
    d_gated_b = jnp.einsum("td,id->ti", d_mixed_b, w_mamba_out, preferred_element_type=fl_type)
    g_gated_gain = jnp.sum(d_gated_b * gated_norm, axis=0)
    d_gated = scale_all * (d_gated_b * mixer_gain - gated_norm * mean_all)
    d_scan = (d_gated * gate_act).astype(bf_type)
    d_gate_raw = d_gated * scan_float * swish_slope(gate_raw)

    g_rows = jnp.concatenate([g_mamba_out, g_attn_out, g_down], axis=0).astype(bf_type)
    g_got = seq_exchange(
        g_rows.reshape(g_rows.shape[0], seq_count, col_width).transpose(1, 0, 2)
    )
    g_out = jnp.concatenate(
        [
            g_got[:, :x_width].reshape(fsdp_count, gain_own, col_width),
            g_got[:, x_width : x_width + query_width].reshape(fsdp_count, attn_own, col_width),
            g_got[:, x_width + query_width :].reshape(fsdp_count, FF // fsdp_count, col_width),
        ],
        axis=1,
    )
    g_out = (
        g_out.reshape(fsdp_count, chunks, own_rows, col_width)
        .transpose(0, 2, 1, 3)
        .reshape(model, chunks * col_width)
    )
    big_shard = lax.psum_scatter(
        jnp.concatenate([g_gate_up.astype(bf_type), g_out], axis=1),
        "fsdp",
        scatter_dimension=0,
        tiled=True,
    )
    big_grads = lax.all_gather(big_shard, "seq", axis=0, tiled=False).astype(fl_type)

    d_att = d_attn.astype(bf_type).reshape(rows, query_share, HD).transpose(1, 0, 2)
    d_weights = jnp.einsum("hid,jd->hij", d_att, value_b, preferred_element_type=fl_type)
    inner_sum = jnp.sum(d_att.astype(fl_type) * attended, axis=-1, keepdims=True)
    d_scores = (weights * (d_weights - inner_sum) * (1.0 / math.sqrt(HD))).astype(bf_type)
    d_queries = jnp.einsum("hij,jd->hid", d_scores, key_b, preferred_element_type=fl_type)
    d_keys = jnp.einsum(
        "hij,hid->jd", d_scores, q_heads.astype(bf_type), preferred_element_type=fl_type
    )
    d_value = jnp.einsum("hij,hid->jd", weights_b, d_att, preferred_element_type=fl_type)
    d_y = d_scan.reshape(rows, head_share, HD).transpose(1, 0, 2)
    d_y_float = d_y.astype(fl_type)
    d_kernel = jnp.einsum("htd,hpd->htp", d_y, x_step, preferred_element_type=fl_type)
    d_inner = jnp.sum(d_kernel * decay, axis=0).astype(bf_type)
    d_x_step = jnp.einsum("htp,htd->hpd", kernel_b, d_y, preferred_element_type=fl_type)
    d_c = jnp.dot(d_inner, b_mat, preferred_element_type=fl_type)
    d_b = jnp.einsum("tp,tn->pn", d_inner, c_mat, preferred_element_type=fl_type)
    d_x = step_t[:, :, None] * d_x_step + skip[:, None, None] * d_y_float
    g_skip = jnp.sum(d_y_float * x_heads, axis=(1, 2))
    d_step_direct = jnp.sum(x_heads * d_x_step, axis=-1)
    d_cum = jnp.sum(d_y_float * scan_y, axis=-1) - jnp.sum(
        x_step.astype(fl_type) * d_x_step, axis=-1
    )
    d_log_step = jnp.dot(d_cum, causal.astype(fl_type), precision=highest)
    (d_conv, d_step, d_query, d_key), grad_params = pull_back(
        (
            jnp.concatenate([d_x.transpose(1, 0, 2).reshape(rows, x_width), d_b, d_c], axis=1),
            d_step_direct.T,
            d_log_step.T,
            d_queries.transpose(1, 0, 2).reshape(rows, query_width),
            d_keys,
        )
    )
    d_in = jnp.concatenate(
        [
            d_gate_raw,
            d_conv,
            d_query,
            d_key,
            d_value,
            d_step,
            jnp.zeros((rows, 128 - head_share), fl_type),
        ],
        axis=1,
    ).astype(bf_type)
    g_in = jnp.einsum("td,tc->dc", normed, d_in, preferred_element_type=fl_type)
    in_shard = lax.psum_scatter(g_in.astype(bf_type), "fsdp", scatter_dimension=0, tiled=True)
    in_grads = lax.all_gather(in_shard, "seq", axis=0, tiled=False).astype(fl_type)
    d_normed = seq_reduce(
        jnp.einsum("tc,dc->td", d_in, in_all, preferred_element_type=fl_type).astype(bf_type)
    )
    first_scale = rms_scale(residual)
    first_norm = residual * first_scale
    g_norm_gain = jnp.sum(d_normed * first_norm, axis=0)
    d_first = d_normed * first_gain
    grad_tok = d_mixed + first_scale * (
        d_first - first_norm * jnp.mean(d_first * first_norm, axis=-1, keepdims=True)
    )

    def placed_cols(block, width, start):
        return lax.dynamic_update_slice_in_dim(
            jnp.zeros(block.shape[:-1] + (width,), fl_type), block, start, block.ndim - 1
        )

    conv_channels = DI + 2 * NST
    taps_bias = jnp.concatenate([grad_params[0], grad_params[1][None]], axis=0)
    taps_total = jnp.concatenate(
        [
            placed_cols(taps_bias[:, :x_width], DI, seq_index * x_width),
            taps_bias[:, x_width:],
        ],
        axis=1,
    )
    heads_total = placed_cols(
        jnp.stack([grad_params[2], grad_params[3], g_skip]), MH, seq_index * head_share
    )
    gated_total = placed_cols(g_gated_gain, DI, seq_index * x_width)
    small = lax.psum(
        jnp.concatenate(
            [
                taps_total.reshape(-1),
                gated_total,
                g_norm_gain,
                g_ffn_gain,
                heads_total.reshape(-1),
            ]
        ),
        ("seq", "fsdp"),
    )
    at = (KC + 1) * conv_channels
    taps_sum = small[:at].reshape(KC + 1, conv_channels)
    fsdp_index = lax.axis_index("fsdp")
    gated_sum = lax.dynamic_slice_in_dim(small, at + fsdp_index * gain_own, gain_own, 0)
    at = at + DI
    norm_sum = lax.dynamic_slice_in_dim(small, at + fsdp_index * own_rows, own_rows, 0)
    at = at + model
    ffn_gain_sum = lax.dynamic_slice_in_dim(small, at + fsdp_index * own_rows, own_rows, 0)
    at = at + model
    heads_sum = small[at : at + 3 * MH].reshape(3, MH)

    def side(array):
        return jnp.concatenate([array[group] for group in range(seq_count)], axis=1)

    def owned(start):
        slots = []
        for kv_head in range(KVH):
            users = [group for group in range(seq_count) if owners[group] == kv_head]
            total = in_grads[users[0]][:, start : start + HD]
            for group in users[1:]:
                total = total + in_grads[group][:, start : start + HD]
            slots.append(total)
        return slots

    q_at = 2 * x_width + 2 * NST
    grad_mamba_in = jnp.concatenate(
        [
            side(in_grads[:, :, :x_width]),
            side(in_grads[:, :, x_width : 2 * x_width]),
            jnp.sum(in_grads[:, :, 2 * x_width : q_at], axis=0),
        ],
        axis=1,
    )
    k_at = q_at + query_width
    grad_attn_in = jnp.concatenate(
        [side(in_grads[:, :, q_at:k_at])] + owned(k_at) + owned(k_at + HD), axis=1
    )
    grad_step_in = side(in_grads[:, :, main_width : main_width + head_share])
    grad_gate_up = jnp.concatenate(
        [side(big_grads[:, :, :ff_width]), side(big_grads[:, :, ff_width : 2 * ff_width])], axis=1
    )
    out_grads = jnp.concatenate(
        [
            side(
                big_grads[
                    :,
                    :,
                    2 * ff_width + at * col_width : 2 * ff_width + (at + 1) * col_width,
                ]
            )
            for at in range(chunks)
        ],
        axis=0,
    )
    return (
        layer_out[None],
        grad_tok[None],
        norm_sum,
        grad_mamba_in,
        grad_step_in,
        grad_attn_in,
        taps_sum[:KC],
        taps_sum[KC],
        heads_sum[0],
        heads_sum[1],
        heads_sum[2],
        gated_sum,
        out_grads[:gain_own],
        out_grads[gain_own : gain_own + attn_own],
        ffn_gain_sum,
        grad_gate_up,
        out_grads[gain_own + attn_own :],
    )


def solution(mesh):
    placed = (
        P("fsdp", "seq", None),
        P("fsdp", "seq", None),
        P("fsdp", None),
        P("fsdp"),
        P("fsdp", None),
        P("fsdp", None),
        P("fsdp", None),
        P(),
        P(),
        P(),
        P(),
        P(),
        P("fsdp"),
        P("fsdp", None),
        P("fsdp", None),
        P("fsdp"),
        P("fsdp", None),
        P("fsdp", None),
    )
    return jax.shard_map(
        shards,
        mesh=mesh,
        in_specs=placed,
        out_specs=(
            P("fsdp", "seq", None),
            P("fsdp", "seq", None),
            P("fsdp"),
            P("fsdp", None),
            P("fsdp", None),
            P("fsdp", None),
            P(),
            P(),
            P(),
            P(),
            P(),
            P("fsdp"),
            P("fsdp", None),
            P("fsdp", None),
            P("fsdp"),
            P("fsdp", None),
            P("fsdp", None),
        ),
        check_vma=False,
    )
```

time: 1740 us -> 620 us (0.36)
  waiting for transfers between devices: 1040 us -> 279 us
  matrix products: 156 us -> 60.2 us
  local copies, waits for them, and re-layouts: 179 us -> 99.7 us
  other arithmetic: 112 us -> 40.9 us
  blocking collectives: 168 us -> 101 us
  starting transfers between devices: 49.9 us -> 12.8 us
    reduce_scatter x7 -> x1, waiting for transfers between devices: 838 us -> 8.11 us  [shards(): lax.psum_scatter(g_in.astype(bf_type), 'fsdp', scatter_dimension=0, tiled...]
    dot_general x66 -> x24, matrix products: 133 us -> 48.1 us  [the longest x1 5.37 us: shards(): g_in = jnp.einsum('td,tc->dc', normed, d_in, preferred_element_type=fl_type)]
    dynamic_update_slice x72 -> x2, local copies, waits for them, and re-layouts: 83.4 us -> 0.39 us  [placed_cols(): lax.dynamic_update_slice_in_dim(jnp.zeros(block.shape[:-1] + (width,), fl...]
    all_gather x3 -> x0, blocking collectives: 67.3 us -> none  [the longest x1 26.5 us: shards(): lax.all_gather(step_in, 'fsdp', axis=0, tiled=True)]
    all_to_all x0 -> x2, blocking collectives: none -> 58.8 us  [seq_exchange(): lax.all_to_all(blocks, 'seq', split_axis=0, concat_axis=0, tiled=True)]
    all_gather x6 -> x8, waiting for transfers between devices: 133 us -> 190 us  [the longest x1 58.6 us: shards(): in_all = lax.all_gather(in_pack, 'fsdp', axis=0, tiled=True)]
    unnamed x2 -> x0, blocking collectives: 53.4 us -> none
    all_to_all x14 -> x3, starting transfers between devices: 49.1 us -> 12 us  [seq_exchange(): lax.all_to_all(blocks, 'seq', split_axis=0, concat_axis=0, tiled=True)]
  transfers between devices with their start and end apart: 28 -> 13, of which waited for: 21 -> 13; matrix products, arithmetic and copies ran while one was open for 15% -> 17% of each run, Pallas kernels for 0% -> 0%
where the time goes in v1:
time: 620 us; the launch traced here: 611 us
  waiting for transfers between devices  279 us (45%)
  blocking collectives  101 us (16%)
  local copies, waits for them, and re-layouts  99.7 us (16%)
  matrix products  60.2 us (10%)
  other arithmetic  40.9 us (7%)
  between operations  16.8 us (3%)
  starting transfers between devices  12.8 us (2%)
    all_to_all x2, blocking collectives, seq_exchange(): lax.all_to_all(blocks, 'seq', split_axis=0, concat_axis=0, tiled=True)  58.8 us
    all_gather x1, waiting for transfers between devices, shards(): in_all = lax.all_gather(in_pack, 'fsdp', axis=0, tiled=True)  58.6 us
    all_gather x1, waiting for transfers between devices, shards(): big_all = lax.all_gather(big_pack, 'fsdp', axis=0, tiled=True)  57.4 us
    psum x1, blocking collectives, shards(): lax.psum(jnp.concatenate([taps_total.reshape(-1), gated_total, g_norm_gai...  42.5 us
    all_to_all x3, waiting for transfers between devices, seq_exchange(): lax.all_to_all(blocks, 'seq', split_axis=0, concat_axis=0, tiled=True)  41.3 us
    all_gather x4, waiting for transfers between devices, seq_gather(): return lax.all_gather(array, 'seq', axis=0, tiled=True)  41.3 us
    unnamed x11, waiting for transfers between devices  40 us
    unnamed x288, local copies, waits for them, and re-layouts  32.3 us
  transfers between devices with their start and end apart: 13, of which 13 were waited for; matrix products, arithmetic and copies ran while one was open for 17% of the time, Pallas kernels for 0%

profile of v1, /device:TPU:0, one launch (start us, length us, event | category | flops | bytes accessed | tf_op | source)
XLA Modules:
  0.0 610.8 jit_solution(12090798967682031050)
XLA Ops:
  26.1 2.9 all-gather.21.cloned.1.call-done
  30.6 58.6 %all-gather.13.cloned.1.call-done = bf16[1024,1408]{1,0:T(8,128)(2,1)} async-done(((bf16[128,1408]{1,0:T(8,128)(2,1)}), bf16[1024,1408]{1,0:T(8,128)(2,1)}) %all-gather.13.cloned.1.call-update) | async-done | bytes 2883600 | tf_op jit(solution)/shard_map/all_gather | solution.py:178
  90.6 3.9 fusion.159
  97.0 2.6 fusion.153
  100.7 2.8 fusion.45
  106.0 57.4 %all-gather.15.cloned.1.call-done = bf16[1024,2048]{1,0:T(8,128)(2,1)} async-done(((bf16[128,2048]{1,0:T(8,128)(2,1)}), bf16[1024,2048]{1,0:T(8,128)(2,1)}) %all-gather.15.cloned.1.call-update) | async-done | bytes 4194320 | tf_op jit(solution)/shard_map/all_gather | solution.py:179
  163.4 3.1 slice.633
  166.5 4.5 reshape.550
  171.0 2.0 copy.436
  174.9 2.3 copy.380
  178.9 2.8 pad_maximum_fusion.1
  181.7 4.6 all-to-all-start
  191.3 2.2 fusion.20
  194.7 2.3 fusion.160
  197.0 15.0 %all-to-all-done = bf16[4,1024,256]{1,2,0:T(8,128)(2,1)} async-done(((bf16[4,1024,256]{1,2,0:T(8,128)(2,1)}), bf16[4,1024,256]{1,2,0:T(8,128)(2,1)}, u32[]{:S(2)}, u32[]{:S(2)}) %all-to-all-start) | async-done | bytes 2097184 | tf_op jit(solution)/shard_map/all_to_all | solution.py:37
  218.5 4.7 concatenate.148
  223.2 30.7 %all_to_all.25 = bf16[4,128,2176]{2,1,0:T(8,128)(2,1)S(1)} all-to-all(bf16[4,128,2176]{2,1,0:T(8,128)(2,1)} %concatenate.148), channel_id=1, replica_groups=mesh['seq'=4,'fsdp'=8] {'seq'}, dimensions={0} | all-to-all | bytes 4456448 | tf_op jit(solution)/shard_map/all_to_all | solution.py:37
  259.4 2.3 slice.655
  261.7 12.3 %all-gather.17.cloned.1.call-done = bf16[512,1152]{1,0:T(8,128)(2,1)} async-done(((bf16[128,1152]{1,0:T(8,128)(2,1)}), bf16[512,1152]{1,0:T(8,128)(2,1)}) %all-gather.17.cloned.1.call-update) | async-done | bytes 1179664 | tf_op jit(solution)/shard_map/all_gather | solution.py:33
  274.0 4.5 fusion.17
  278.5 13.6 %all-gather.23.cloned.1.call-done = bf16[1,512,1024]{2,1,0:T(8,128)(2,1)} async-done(((bf16[1,128,1024]{2,1,0:T(8,128)(2,1)}), bf16[1,512,1024]{2,1,0:T(8,128)(2,1)}) %all-gather.23.cloned.1.call-update) | async-done | bytes 1048592 | tf_op jit(solution)/shard_map/all_gather | solution.py:33
  292.1 3.4 multiply_convert_fusion.5
  298.0 28.1 %all_to_all.26 = bf16[4,128,2048]{2,1,0:T(8,128)(2,1)S(1)} all-to-all(bf16[4,128,2048]{2,1,0:T(8,128)(2,1)S(1)} %bitcast.345), channel_id=1, replica_groups=mesh['seq'=4,'fsdp'=8] {'seq'}, dimensions={0} | all-to-all | bytes 4194304 | tf_op jit(solution)/shard_map/all_to_all | solution.py:37
  335.9 12.4 %all-gather.19.cloned.1.call-done = bf16[512,1152]{1,0:T(8,128)(2,1)} async-done(((bf16[128,1152]{1,0:T(8,128)(2,1)}), bf16[512,1152]{1,0:T(8,128)(2,1)}) %all-gather.19.cloned.1.call-update) | async-done | bytes 1179664 | tf_op jit(solution)/shard_map/all_gather | solution.py:33
  349.5 4.4 multiply_convert_fusion.8
  354.0 2.3 multiply_reduce_fusion
  365.8 2.6 multiply_reduce_fusion.4
  374.1 3.5 concatenate.154
  377.6 5.4 convolution_convert_fusion
  383.0 2.2 convolution_convert_fusion.5
  393.4 3.7 all-to-all-start.4
  397.2 4.0 convolution_convert_fusion.1
  401.2 21.6 %all-to-all-done.4 = bf16[4,1024,256]{2,1,0:T(8,128)(2,1)S(1)} async-done(((bf16[4,1024,256]{2,1,0:T(8,128)(2,1)}), bf16[4,1024,256]{2,1,0:T(8,128)(2,1)S(1)}, u32[]{:S(2)}, u32[]{:S(2)}) %all-to-all-start.4) | async-done | bytes 2097184 | tf_op jit(solution)/shard_map/all_to_all | solution.py:37
  423.1 2.6 copy.402
  425.7 2.4 copy.452
  428.1 2.5 pad_maximum_fusion
  430.6 6.5 %copy.437 = bf16[1024,2048]{1,0:T(8,128)(2,1)} copy(bf16[1024,2048]{0,1:T(8,128)(2,1)} %pad_maximum_fusion) | data formatting | bytes 8388608
  438.4 4.9 convolution_convert_fusion.3
  443.4 3.7 all-to-all-start.3
  447.3 8.1 %reduce-scatter.5.cloned.1.call-done = bf16[128,1408]{1,0:T(8,128)(2,1)} async-done(((bf16[1024,1408]{1,0:T(8,128)(2,1)}), bf16[128,1408]{1,0:T(8,128)(2,1)}) %reduce-scatter.5.cloned.1.call-update) | async-done | bytes 360464 | tf_op jit(solution)/shard_map/reduce_scatter | solution.py:411
  456.8 4.7 all-to-all-done.3
  462.6 42.5 %psum.7 = f32[12616]{0:T(1024)S(1)} all-reduce(f32[12616]{0:T(1024)S(1)} %constant_dynamic-update-slice_fusion.2), channel_id=1, replica_groups=mesh['seq'=4,'fsdp'=8] {'seq','fsdp'}, use_global_device_ids=true, to_apply=%region_28.29 | all-reduce | flops 12616 | bytes 100928 | tf_op jit(solution)/shard_map/psum | solution.py:442
  507.6 2.1 fusion.58
  509.7 38.7 %reduce-scatter.7.cloned.1.call-done = bf16[128,2048]{1,0:T(8,128)(2,1)} async-done(((bf16[1024,2048]{1,0:T(8,128)(2,1)}), bf16[128,2048]{1,0:T(8,128)(2,1)}) %reduce-scatter.7.cloned.1.call-update) | async-done | bytes 524304
  548.4 2.0 copy.438
  551.0 17.5 %all-gather.25.cloned.1.call-done = bf16[512,1408]{1,0:T(8,128)(2,1)} async-done(((bf16[128,1408]{1,0:T(8,128)(2,1)}), bf16[512,1408]{1,0:T(8,128)(2,1)}) %all-gather.25.cloned.1.call-update) | async-done | bytes 1441808 | tf_op jit(solution)/shard_map/all_gather | solution.py:412
  578.2 15.1 %all-gather.27.cloned.1.call-done = bf16[512,2048]{0,1:T(8,128)(2,1)} async-done(((bf16[128,2048]{0,1:T(8,128)(2,1)}), bf16[512,2048]{0,1:T(8,128)(2,1)}) %all-gather.27.cloned.1.call-update) | async-done | bytes 2097168 | tf_op jit(solution)/shard_map/all_gather | solution.py:364
  593.3 4.2 copy.439
  (473 shorter events, 108.0 us)
Async XLA Ops:
  7.2 8.5 %copy-start = (bf16[64,1024]{1,0:T(8,128)(2,1)S(1)}, bf16[64,1024]{1,0:T(8,128)(2,1)}, u32[]{:S(2)}) copy-start(bf16[64,1024]{1,0:T(8,128)(2,1)} %param.32) | copy-start | bytes 393220
  7.2 21.8 %all-gather.21.cloned.1.call-start = ((), (), s32[]{:S(2)}) async-start(), calls=%async_computation.12 | async-start | bytes 1310720 | tf_op jit(solution)/shard_map/all_gather | solution.py:33
  7.9 81.2 %all-gather.13.cloned.1.call-start = ((), (), s32[]{:S(2)}) async-start(), calls=%async_computation.7 | async-start | bytes 3244032 | tf_op jit(solution)/shard_map/all_gather | solution.py:178
  8.0 15.4 %copy-start.112 = (f32[24]{0:T(128)S(1)}, f32[24]{0:T(128)}, u32[]{:S(2)}) copy-start(f32[24]{0:T(128)} %param.29) | copy-start | bytes 292
  8.0 15.4 %copy-start.113 = (f32[24]{0:T(128)S(1)}, f32[24]{0:T(128)}, u32[]{:S(2)}) copy-start(f32[24]{0:T(128)} %param.27) | copy-start | bytes 292
  8.0 15.5 %copy-start.56 = (s32[1,512]{1,0:T(1,128)S(1)}, s32[1,512]{1,0:T(1,128)}, u32[]{:S(2)}) copy-start(s32[1,512]{1,0:T(1,128)} %param.20) | copy-start | bytes 6148
  14.7 9.4 %copy-start.78 = (f32[4,1792]{1,0:T(4,128)S(1)}, f32[4,1792]{1,0:T(4,128)}, u32[]{:S(2)}) copy-start(f32[4,1792]{1,0:T(4,128)} %param.25) | copy-start | bytes 86020
  14.7 9.5 %slice-start = ((f32[4,1792]{1,0:T(4,128)}), f32[4,256]{1,0:T(4,128)S(1)}, s32[]{:S(2)}) async-start(f32[4,1792]{1,0:T(4,128)} %param.25), calls=%async_computation.17 | async-start | bytes 8192 | tf_op jit(solution)/shard_map/slice | solution.py:231
  14.7 9.5 %copy-start.105 = (f32[24]{0:T(128)S(1)}, f32[24]{0:T(128)}, u32[]{:S(2)}) copy-start(f32[24]{0:T(128)} %param.28) | copy-start | bytes 292
  15.7 147.7 %all-gather.15.cloned.1.call-start = ((), (), s32[]{:S(2)}) async-start(), calls=%async_computation.8 | async-start | bytes 4718592 | tf_op jit(solution)/shard_map/all_gather | solution.py:179
  23.4 77.2 %copy-start.116 = (f32[6]{0:T(128)}, f32[6]{0:T(128)S(1)}, u32[]{:S(2)}) copy-start(f32[6]{0:T(128)S(1)} %dynamic_slice.70) | copy-start | bytes 76
  23.5 76.3 %copy-start.99 = (f32[6]{0:T(128)}, f32[6]{0:T(128)S(1)}, u32[]{:S(2)}) copy-start(f32[6]{0:T(128)S(1)} %dynamic_slice.69) | copy-start | bytes 76
  23.7 169.7 %copy-start.32 = (pred[512,512]{0,1:T(8,128)(4,1)}, pred[512,512]{0,1:T(8,128)(4,1)S(1)}, u32[]{:S(2)}) copy-start(pred[512,512]{0,1:T(8,128)(4,1)S(1)} %fusion.36) | copy-start | bytes 786436
  24.2 76.5 %copy-start.48 = (pred[512,512]{1,0:T(8,128)(4,1)}, pred[512,512]{1,0:T(8,128)(4,1)S(1)}, u32[]{:S(2)}) copy-start(pred[512,512]{1,0:T(8,128)(4,1)S(1)} %copy.373) | copy-start | bytes 786436
  24.2 71.6 %copy-start.62 = (f32[640]{0:T(1024)}, f32[640]{0:T(1024)S(1)}, u32[]{:S(2)}) copy-start(f32[640]{0:T(1024)S(1)} %get-tuple-element.103) | copy-start | bytes 7684
  24.2 71.6 %copy-start.64 = (f32[640]{0:T(1024)}, f32[640]{0:T(1024)S(1)}, u32[]{:S(2)}) copy-start(f32[640]{0:T(1024)S(1)} %get-tuple-element.101) | copy-start | bytes 7684
  24.4 75.6 %copy-start.114 = (f32[6]{0:T(128)}, f32[6]{0:T(128)S(1)}, u32[]{:S(2)}) copy-start(f32[6]{0:T(128)S(1)} %fusion.144) | copy-start | bytes 76
  25.7 68.8 %copy-start.66 = (f32[512]{0:T(512)}, f32[512]{0:T(512)S(1)}, u32[]{:S(2)}) copy-start(f32[512]{0:T(512)S(1)} %subtract_convert_fusion.1) | copy-start | bytes 6148
  25.8 70.1 %copy-start.87 = (pred[512]{0:T(512)(128)(4,1)}, pred[512]{0:T(512)(128)(4,1)S(1)}, u32[]{:S(2)}) copy-start(pred[512]{0:T(512)(128)(4,1)S(1)} %get-tuple-element.183) | copy-start | bytes 1540
  25.8 70.1 %copy-start.89 = (pred[512]{0:T(512)(128)(4,1)}, pred[512]{0:T(512)(128)(4,1)S(1)}, u32[]{:S(2)}) copy-start(pred[512]{0:T(512)(128)(4,1)S(1)} %get-tuple-element.184) | copy-start | bytes 1540
  25.8 70.1 %copy-start.91 = (pred[512]{0:T(512)(128)(4,1)}, pred[512]{0:T(512)(128)(4,1)S(1)}, u32[]{:S(2)}) copy-start(pred[512]{0:T(512)(128)(4,1)S(1)} %get-tuple-element.185) | copy-start | bytes 1540
  30.5 64.0 %copy-start.102 = (f32[512]{0:T(512)}, f32[512]{0:T(512)S(1)}, u32[]{:S(2)}) copy-start(f32[512]{0:T(512)S(1)} %add_rsqrt_fusion) | copy-start | bytes 6148
  94.5 9.0 %copy-start.55 = (f32[512,1408]{0,1:T(8,128)}, f32[512,1408]{0,1:T(8,128)S(1)}, u32[]{:S(2)}) copy-start(f32[512,1408]{0,1:T(8,128)S(1)} %get-tuple-element.187) | copy-start | bytes 8650756
  181.7 30.3 %all-to-all-start = ((bf16[4,1024,256]{1,2,0:T(8,128)(2,1)}), bf16[4,1024,256]{1,2,0:T(8,128)(2,1)}, u32[]{:S(2)}, u32[]{:S(2)}) async-start(bf16[4,1024,256]{1,2,0:T(8,128)(2,1)} %pad_maximum_fusion.1), calls=%async_computation | async-start | bytes 4194304 | tf_op jit(solution)/shard_map/all_to_all | solution.py:37
  186.3 87.7 %all-gather.17.cloned.1.call-start = ((), (), s32[]{:S(2)}) async-start(), calls=%async_computation.9 | async-start | bytes 1474560 | tf_op jit(solution)/shard_map/all_gather | solution.py:33
  197.0 18.2 %copy-start.43 = (bf16[2,512,64]{1,2,0:T(8,128)(2,1)S(1)}, bf16[2,512,64]{1,2,0:T(8,128)(2,1)}, u32[]{:S(2)}) copy-start(bf16[2,512,64]{1,2,0:T(8,128)(2,1)} %get-tuple-element.192) | copy-start | bytes 393220
  197.0 19.6 %copy-start.17 = (f32[512,384]{0,1:T(8,128)S(1)}, f32[512,384]{0,1:T(8,128)}, u32[]{:S(2)}) copy-start(f32[512,384]{0,1:T(8,128)} %get-tuple-element.118) | copy-start | bytes 2359300
  197.0 19.6 %copy-start.82 = (f32[384]{0:T(512)S(1)}, f32[384]{0:T(512)}, u32[]{:S(2)}) copy-start(f32[384]{0:T(512)} %dynamic-slice_convert_fusion) | copy-start | bytes 4612
  257.5 69.0 %copy-start.79 = (f32[128]{0:T(128)}, f32[128]{0:T(128)S(1)}, u32[]{:S(2)}) copy-start(f32[128]{0:T(128)S(1)} %add_rsqrt_fusion.2) | copy-start | bytes 1540
  257.9 20.6 %copy-start.47 = (bf16[128,126]{1,0:T(8,128)(2,1)}, bf16[128,126]{1,0:T(8,128)(2,1)S(1)}, u32[]{:S(2)}) copy-start(bf16[128,126]{1,0:T(8,128)(2,1)S(1)} %broadcast.267) | copy-start | bytes 96772
  258.8 33.4 %all-gather.23.cloned.1.call-start = ((), (), s32[]{:S(2)}) async-start(), calls=%async_computation.13 | async-start | bytes 1310720 | tf_op jit(solution)/shard_map/all_gather | solution.py:33
  259.4 89.0 %all-gather.19.cloned.1.call-start = ((), (), s32[]{:S(2)}) async-start(), calls=%async_computation.10 | async-start | bytes 1474560 | tf_op jit(solution)/shard_map/all_gather | solution.py:33
  330.7 124.6 %reduce-scatter.5.cloned.1.call-start = ((), (), s32[]{:S(2)}) async-start(), calls=%async_computation.11 | async-start | bytes 3244032 | tf_op jit(solution)/shard_map/reduce_scatter | solution.py:411
  335.9 18.1 %copy-start.95 = (f32[512]{0:T(512)}, f32[512]{0:T(512)S(1)}, u32[]{:S(2)}) copy-start(f32[512]{0:T(512)S(1)} %fusion.82) | copy-start | bytes 6148
  393.4 29.4 %all-to-all-start.4 = ((bf16[4,1024,256]{2,1,0:T(8,128)(2,1)}), bf16[4,1024,256]{2,1,0:T(8,128)(2,1)S(1)}, u32[]{:S(2)}, u32[]{:S(2)}) async-start(bf16[4,1024,256]{2,1,0:T(8,128)(2,1)} %maximum_bitcast_fusion), calls=%async_computation.5 | async-start | bytes 4194304 | tf_op jit(solution)/shard_map/all_to_all | solution.py:37
  397.2 151.2 %reduce-scatter.7.cloned.1.call-start = ((), (), s32[]{:S(2)}) async-start(), calls=%async_computation.16 | async-start | bytes 4718592
  443.3 12.2 %copy-start.106 = (f32[24]{0:T(128)S(1)}, f32[24]{0:T(128)}, u32[]{:S(2)}) copy-start(f32[24]{0:T(128)} %param.28) | copy-start | bytes 292
  443.3 12.2 %copy-start.107 = (f32[6]{0:T(128)S(1)}, f32[6]{0:T(128)}, u32[]{:S(2)}) copy-start(f32[6]{0:T(128)} %get-tuple-element.180) | copy-start | bytes 76
  443.3 12.3 %copy-start.101 = (f32[6]{0:T(128)S(1)}, f32[6]{0:T(128)}, u32[]{:S(2)}) copy-start(f32[6]{0:T(128)} %get-tuple-element.96) | copy-start | bytes 76
  443.3 12.3 %copy-start.104 = (f32[6]{0:T(128)S(1)}, f32[6]{0:T(128)}, u32[]{:S(2)}) copy-start(f32[6]{0:T(128)} %get-tuple-element.104) | copy-start | bytes 76
  443.4 12.5 %copy-start.103 = (f32[384]{0:T(512)S(1)}, f32[384]{0:T(512)}, u32[]{:S(2)}) copy-start(f32[384]{0:T(512)} %get-tuple-element.157) | copy-start | bytes 4612
  443.4 18.1 %all-to-all-start.3 = ((bf16[4,128,1024]{2,1,0:T(8,128)(2,1)}), bf16[4,128,1024]{2,1,0:T(8,128)(2,1)S(1)}, u32[]{:S(2)}, u32[]{:S(2)}) async-start(bf16[4,128,1024]{2,1,0:T(8,128)(2,1)} %bitcast.366), calls=%async_computation.3 | async-start | bytes 2097152 | tf_op jit(solution)/shard_map/all_to_all | solution.py:37
  447.0 15.5 %copy-start.70 = (f32[1024]{0:T(1024)S(1)}, f32[1024]{0:T(1024)}, u32[]{:S(2)}) copy-start(f32[1024]{0:T(1024)} %get-tuple-element.87) | copy-start | bytes 12292
  447.0 60.5 %copy-start.10 = (f32[128,2048]{1,0:T(8,128)S(1)}, f32[128,2048]{1,0:T(8,128)}, u32[]{:S(2)}) copy-start(f32[128,2048]{1,0:T(8,128)} %copy-done.9) | copy-start | bytes 3145732
  447.1 60.5 %copy-start.80 = (f32[128]{0:T(128)S(1)}, f32[128]{0:T(128)}, u32[]{:S(2)}) copy-start(f32[128]{0:T(128)} %copy-done.79) | copy-start | bytes 1540
  447.1 60.5 %copy-start.98 = (f32[128]{0:T(128)S(1)}, f32[128]{0:T(128)}, u32[]{:S(2)}) copy-start(f32[128]{0:T(128)} %copy-done.97) | copy-start | bytes 1540
  447.1 121.4 %all-gather.25.cloned.1.call-start = ((), (), s32[]{:S(2)}) async-start(), calls=%async_computation.14 | async-start | bytes 1802240 | tf_op jit(solution)/shard_map/all_gather | solution.py:412
  455.4 137.9 %all-gather.27.cloned.1.call-start = ((), (), s32[]{:S(2)}) async-start(), calls=%async_computation.15 | async-start | bytes 2621440 | tf_op jit(solution)/shard_map/all_gather | solution.py:364
  (94 other events, 244.1 us)
Sparse Core Ops, SparseCore 0:
  9.6 19.4 all-gather.20
  31.8 57.2 all-gather.12
  91.8 71.5 all-gather.14
  258.9 15.0 all-gather.16
  275.4 16.6 all-gather.22
  330.9 17.4 all-gather.18
  383.1 72.1 reduce-scatter.4
  459.0 89.3 reduce-scatter.6
  549.9 18.5 all-gather.24
  570.5 22.8 all-gather.26
